TPU v7x, 128 devices: a whole 4x4x4 slice. The times are simulated.
128 devices in a mesh: row: 4 (over y_lo, core), col: 32 (over z, y_hi, x).
Axes of the slice: x: 4, y: 4 (y_hi: 2, y_lo: 2; y = y_hi * 2 + y_lo), z: 4, core: 2. Of those that a mesh axis runs over, the one named last changes fastest.
Arguments:
- matrix_tiles: float32 [4, 32, 4, 256, 256], P('row', 'col'), as said below
- tile_rows: int32 [4, 32, 4], P('row', 'col'), may hold values from 0 to 7, as said below
- keep_rows: int32 [4, 32, 4], P('row', 'col'), may hold values from 0 to 7, as said below
- owners: int32 [4, 128, 1], P('row', 'col'), may hold values from 0 to 3; in each aligned block of 4 rows (0 to 3, 4 to 7, ..., all dimensions but the last counted through in order) at most 2 rows name the same one
Outputs:
- owned: float32 [4, 32, 8, 256, 256], P('row', 'col')
Inputs may be any that keep to these rules, and one draw needn't show every extreme that they name: `matrix_tiles`: every entry is positive. `tile_rows`: for each r and tile column j the 4 entries are distinct, and include j % 8 where j // 8 == r. `keep_rows`: for each r and tile column j the 4 entries are distinct, and include j % 8 where j // 8 == r. `owners`: among the 4 kept tiles of one row block and one column block, at most 2 go to the same owner.
All inputs are finite; a program needn't handle non-finite values.
Results may differ from a plain program's by a relative error of at most 0.000071.
Values sent between devices are 32-bit elements; how exact they have to be, the bound alone decides.
A program may use at most 192 MiB of HBM per device.

v0:
```python
import jax
import jax.numpy as jnp
from jax import lax
from jax.sharding import PartitionSpec as P

TR = 8
KEEP = 4


def from_root(x, axis, root):
    mine = lax.axis_index(axis) == root
    return lax.psum(jnp.where(mine, x, jnp.zeros_like(x)), axis)


def section_product(running, a_panel, a_levels, b_panel, b_levels, section_index):
    columns = section_index * TR + b_levels
    chosen = jnp.take(a_panel, columns, axis=0)
    chosen_levels = jnp.take(a_levels, columns, axis=0)
    products = jnp.einsum("jzyab,jzbc->jzyac", chosen, b_panel, precision=lax.Precision.HIGHEST)
    selector = (chosen_levels[..., None] == jnp.arange(TR, dtype=jnp.int32)).astype(jnp.float32)
    return running + jnp.einsum(
        "jzyl,jzyac->ljac", selector, products, precision=lax.Precision.HIGHEST
    )


def on_device(matrix_tiles, tile_rows, keep_rows, owners):
    blocks = matrix_tiles.shape[1]
    width = matrix_tiles.shape[3]
    row_count = lax.axis_size("row")
    a_panel, a_levels = (
        lax.all_gather(matrix_tiles, "col", axis=1, tiled=True),
        lax.all_gather(tile_rows, "col", axis=1, tiled=True),
    )
    a_panel = a_panel[0]
    a_levels = a_levels[0]
    expanded = jnp.zeros((TR, blocks, width, width), jnp.float32)
    for section_index in range(row_count):
        b_panel, b_levels = (
            from_root(matrix_tiles[0], "row", section_index),
            from_root(tile_rows[0], "row", section_index),
        )
        expanded = section_product(expanded, a_panel, a_levels, b_panel, b_levels, section_index)
    kept = expanded[keep_rows[0], jnp.arange(blocks, dtype=jnp.int32)[:, None]]
    inflated = kept * kept
    flat = inflated.reshape(blocks * KEEP, width, width)
    column_ids = jnp.repeat(jnp.arange(blocks, dtype=jnp.int32), KEEP)
    most = blocks * KEEP // 2
    slots = row_count * most
    targets = owners[0, :, 0]
    items = targets.shape[0]
    order = jnp.arange(items, dtype=jnp.int32)
    earlier = jnp.sum(
        ((targets[None, :] == targets[:, None]) & (order[None, :] < order[:, None])).astype(
            jnp.int32
        ),
        axis=1,
    )
    slot_index = targets * most + earlier
    placing = slot_index[:, None] == jnp.arange(slots, dtype=jnp.int32)[None, :]
    outgoing = jnp.einsum(
        "fs,fab->sab", placing.astype(jnp.float32), flat, precision=lax.Precision.HIGHEST
    )
    outgoing_ids = jnp.sum(placing.astype(jnp.int32) * (column_ids[:, None] + 1), axis=0) - 1
    arrived, arrived_ids = (
        lax.all_to_all(outgoing, "row", split_axis=0, concat_axis=0, tiled=True),
        lax.all_to_all(outgoing_ids, "row", split_axis=0, concat_axis=0, tiled=True),
    )
    selector = (arrived_ids[:, None] == jnp.arange(blocks, dtype=jnp.int32)[None, :]).astype(
        jnp.float32
    )
    partial_sums = jnp.einsum("sj,sab->jb", selector, arrived, precision=lax.Precision.HIGHEST)
    totals = lax.psum(partial_sums, "row")
    denominators = jnp.einsum("sj,jb->sb", selector, totals, precision=lax.Precision.HIGHEST)
    present = arrived_ids >= 0
    safe_totals = jnp.where(present[:, None], denominators, 1.0)
    order_scale = float(row_count * TR * width)
    owned = order_scale * arrived / safe_totals[:, None, :]
    return owned[None, None]


def solution(mesh):
    placed = (
        P("row", "col", None, None, None),
        P("row", "col", None),
        P("row", "col", None),
        P("row", "col", None),
    )
    return jax.shard_map(
        on_device,
        mesh=mesh,
        in_specs=placed,
        out_specs=P("row", "col", None, None, None),
        check_vma=False,
    )
```

profile of v0, /device:TPU:1, one launch (start us, length us, event | category | flops | bytes accessed | tf_op | source)
XLA Modules:
  0.0 399.6 jit_solution(10358814323807009863)
XLA Ops:
  7.4 0.0 all-gather.2.cloned.1.call-start
  7.4 0.7 all-gather.2.cloned.1.call-update
  8.1 0.0 all-reduce.5.cloned.1.call-start
  8.2 0.0 copy-start.7
  8.2 0.0 copy-start.6
  8.2 0.0 copy-start.8
  8.2 3.4 select_bitcast_fusion.3
  11.5 0.0 all-reduce.5.cloned.1.call-update
  11.6 0.0 copy-done.7
  11.6 0.2 convert_reduce_fusion.1
  11.8 0.1 convert_reduce_fusion
  11.9 0.7 sub.6
  12.5 4.5 %all-to-all-start.1 = ((s32[4,2,1]{1,2,0:T(1,128)}), s32[4,2,1]{1,2,0:T(1,128)S(1)}, u32[]{:S(2)}, u32[]{:S(2)}) async-start(s32[4,2,1]{1,2,0:T(1,128)} %bitcast.71), calls=%async_computation.1 | async-start | bytes 4096 | tf_op jit(solution)/shard_map/all_to_all | solution.py:66
  17.1 0.0 copy-done.6
  17.1 4.2 %all-reduce.1 = (s32[1,4]{1,0:T(1,128)S(1)}, s32[1,4]{1,0:T(1,128)S(1)}, s32[1,4]{1,0:T(1,128)S(1)}, s32[1,4]{1,0:T(1,128)S(1)}) all-reduce(s32[1,4]{1,0:T(1,128)S(1)} %get-tuple-element.23, s32[1,4]{1,0:T(1,128)S(1)} %get-tuple-element.24, s32[1,4]{1,0:T(1,128)S(1)} %get-tuple-element.22, ...), channel_id=1, replica_groups=mesh['row'=4,'col'=32] {'row'}, use_global_device_ids=true, to_apply=%region_7.10 | all-reduce | flops 16 | bytes 128 | tf_op jit(solution)/shard_map/psum | solution.py:12
  21.3 81.7 %all_gather.7 = s32[1,32,4]{2,0,1:T(1,128)S(1)} all-gather(s32[1,1,4]{2,0,1:T(1,128)S(1)} %bitcast.178), channel_id=1, replica_groups=mesh['row'=4,'col'=32] {'col'}, dimensions={1}, use_global_device_ids=true | all-gather | bytes 528 | tf_op jit(solution)/shard_map/all_gather | solution.py:32
  103.0 0.1 copy.67
  103.1 0.1 copy.68
  103.2 0.6 gather_fusion.4
  103.8 0.1 fusion.47
  103.9 0.1 copy.72
  104.0 0.6 gather_fusion.6
  104.6 0.1 fusion.46
  104.6 0.1 copy.75
  104.7 0.6 gather_fusion.8
  105.3 0.1 fusion.45
  105.4 0.1 copy.78
  105.5 0.6 gather_fusion.2
  106.0 0.1 fusion.48
  106.1 0.1 copy.69
  106.2 0.0 copy-done.8
  106.2 180.2 %all-gather.2.cloned.1.call-done = f32[1,32,4,256,256]{4,3,2,0,1:T(8,128)} async-done(((f32[1,1,4,256,256]{4,3,2,0,1:T(8,128)}), f32[1,32,4,256,256]{4,3,2,0,1:T(8,128)}) %all-gather.2.cloned.1.call-update) | async-done | bytes 33554448 | tf_op jit(solution)/shard_map/all_gather | solution.py:31
  286.4 4.9 %gather_fusion.3 = f32[4,4,256,256]{3,2,1,0:T(8,128)} fusion(f32[32,4,256,256]{3,2,1,0:T(8,128)} %bitcast.171, s32[1024]{0:T(1024)S(1)} %pad_clamp_fusion.2), kind=kCustom, calls=%fused_computation.2.clone | custom fusion | bytes 8388624 | tf_op jit(solution)/shard_map/jit(_take)/gather | solution.py:17
  291.3 4.9 %gather_fusion.5 = f32[4,4,256,256]{3,2,1,0:T(8,128)} fusion(f32[32,4,256,256]{3,2,1,0:T(8,128)} %bitcast.172, s32[1024]{0:T(1024)S(1)} %pad_clamp_fusion.1), kind=kCustom, calls=%fused_computation.3.clone | custom fusion | bytes 8388624 | tf_op jit(solution)/shard_map/jit(_take)/gather | solution.py:17
  296.2 4.9 %gather_fusion.1 = f32[4,4,256,256]{3,2,1,0:T(8,128)} fusion(f32[32,4,256,256]{3,2,1,0:T(8,128)} %bitcast.173, s32[1024]{0:T(1024)S(1)} %pad_clamp_fusion.3), kind=kCustom, calls=%fused_computation.clone | custom fusion | bytes 8388624 | tf_op jit(solution)/shard_map/jit(_take)/gather | solution.py:17
  301.2 5.0 %gather_fusion.7 = f32[4,4,256,256]{3,2,1,0:T(8,128)} fusion(f32[32,4,256,256]{3,2,1,0:T(8,128)} %bitcast.174, s32[1024]{0:T(1024)S(1)} %pad_clamp_fusion), kind=kCustom, calls=%fused_computation.4.clone | custom fusion | bytes 8388624 | tf_op jit(solution)/shard_map/jit(_take)/gather | solution.py:17
  306.2 6.5 %fusion.4 = f32[4,4,256,256]{3,2,1,0:T(8,128)S(1)} fusion(f32[4,4,256,256]{3,2,1,0:T(8,128)} %gather_fusion.3, pred[4]{0:T(512)(128)(4,1)S(1)} %get-tuple-element.27, f32[4,256,256]{2,1,0:T(8,128)} %get-tuple-element.15), kind=kOutput, calls=%fused_computation.15 | convolution fusion | flops 3222274048 | bytes 9437188 | tf_op jit(solution)/shard_map/jzyab,jzbc->jzyac/dot_general | solution.py:19
  312.7 5.7 %fusion.12 = f32[256,256,8,1]{1,2,3,0:T(8,128)S(1)} fusion(f32[4,4,256,256]{3,2,1,0:T(8,128)S(1)} %fusion.4, s32[4,4]{0,1:T(4,128)S(1)} %copy.72), kind=kOutput, calls=%fused_computation.25 | convolution fusion | flops 100663424 | bytes 6291520 | tf_op jit(solution)/shard_map/jzyl,jzyac->ljac/dot_general | solution.py:21
  318.4 3.9 fusion.2
  322.3 5.9 %fusion.10 = f32[256,256,8,1]{1,2,3,0:T(8,128)S(1)} fusion(f32[4,4,256,256]{3,2,1,0:T(8,128)S(1)} %fusion.2, s32[4,4]{0,1:T(4,128)S(1)} %copy.75), kind=kOutput, calls=%fused_computation.23 | convolution fusion | flops 100663424 | bytes 6291520 | tf_op jit(solution)/shard_map/jzyl,jzyac->ljac/dot_general | solution.py:21
  328.2 0.0 copy-done.1
  328.2 0.0 copy-done.4
  328.2 0.0 copy-start
  328.2 0.0 copy-start.3
  328.2 4.3 %fusion.6 = f32[4,4,256,256]{3,2,1,0:T(8,128)S(1)} fusion(f32[4,4,256,256]{3,2,1,0:T(8,128)S(1)} %copy-done.1, pred[4]{0:T(512)(128)(4,1)S(1)} %get-tuple-element.28, f32[4,256,256]{2,1,0:T(8,128)S(1)} %copy-done.4), kind=kOutput, calls=%fused_computation.18 | convolution fusion | flops 3222274048 | bytes 9437188 | tf_op jit(solution)/shard_map/jzyab,jzbc->jzyac/dot_general | solution.py:19
  332.6 4.3 %fusion = f32[4,4,256,256]{3,2,1,0:T(8,128)S(1)} fusion(f32[4,4,256,256]{3,2,1,0:T(8,128)S(1)} %copy-done, pred[4]{0:T(512)(128)(4,1)S(1)} %get-tuple-element.25, f32[4,256,256]{2,1,0:T(8,128)S(1)} %copy-done.3), kind=kOutput, calls=%fused_computation.9 | convolution fusion | flops 3222274048 | bytes 9437188 | tf_op jit(solution)/shard_map/jzyab,jzbc->jzyac/dot_general | solution.py:19
  336.9 6.0 %fusion.8 = f32[256,256,8,1]{1,2,3,0:T(8,128)S(1)} fusion(f32[4,4,256,256]{3,2,1,0:T(8,128)S(1)} %fusion, s32[4,4]{0,1:T(4,128)S(1)} %copy.78), kind=kOutput, calls=%fused_computation.21 | convolution fusion | flops 100663424 | bytes 6291520 | tf_op jit(solution)/shard_map/jzyl,jzyac->ljac/dot_general | solution.py:21
  342.9 6.3 %fusion.16 = f32[8,1,256,256]{3,0,2,1:T(8,128)S(1)} fusion(f32[256,256,8,1]{1,2,3,0:T(8,128)S(1)} %fusion.8, f32[256,256,8,1]{1,2,3,0:T(8,128)S(1)} %fusion.10, f32[256,256,8,1]{1,2,3,0:T(8,128)S(1)} %fusion.12, f32[4,4,256,256]{3,2,1,0:T(8,128)S(1)} %fusion.6, s32[4,4]{0,1:T(4,128)S(1)} %copy.69), kind=kOutput, calls=%fused_computation.30 | convolution fusion | flops 102236288 | bytes 12582976 | tf_op jit(solution)/shard_map/jzyl,jzyac->ljac/dot_general | solution.py:21
  349.2 0.7 copy.80
  349.9 0.6 gather_fusion
  350.5 0.1 mul.27
  350.7 1.9 fusion.31
  352.6 2.0 copy.82
  354.6 0.0 all-to-all-done.1
  354.6 4.8 %all-to-all-start = ((f32[8,256,256]{2,1,0:T(8,128)}), f32[8,256,256]{2,1,0:T(8,128)S(1)}, u32[]{:S(2)}, u32[]{:S(2)}) async-start(f32[8,256,256]{2,1,0:T(8,128)} %copy.82), calls=%async_computation | async-start | bytes 4194304 | tf_op jit(solution)/shard_map/all_to_all | solution.py:65
  359.4 0.1 reshape.478
  359.5 0.1 reshape.344
  359.6 0.1 ge.23
  359.6 24.5 %all-to-all-done = f32[8,256,256]{2,1,0:T(8,128)S(1)} async-done(((f32[8,256,256]{2,1,0:T(8,128)}), f32[8,256,256]{2,1,0:T(8,128)S(1)}, u32[]{:S(2)}, u32[]{:S(2)}) %all-to-all-start) | async-done | bytes 2097184 | tf_op jit(solution)/shard_map/all_to_all | solution.py:65
  384.2 0.1 reduce_sum.29
  384.3 0.1 fusion.65
  384.4 5.9 %psum.71 = f32[256]{0:T(256)S(1)} all-reduce(f32[256]{0:T(256)S(1)} %bitcast.177), channel_id=1, replica_groups=mesh['row'=4,'col'=32] {'row'}, use_global_device_ids=true, to_apply=%region_11.14 | all-reduce | flops 256 | bytes 2048 | tf_op jit(solution)/shard_map/psum | solution.py:72
  390.3 0.1 multiply_select_fusion
  390.4 1.6 divide_bitcast_fusion
  (25 shorter events, 0.1 us)
Async XLA Ops:
  7.4 279.0 %all-gather.2.cloned.1.call-start = ((), (), s32[]{:S(2)}) async-start(), calls=%async_computation.2 | async-start | bytes 34603008 | tf_op jit(solution)/shard_map/all_gather | solution.py:31
  8.1 298.1 %all-reduce.5.cloned.1.call-start = ((), (), s32[]{:S(2)}) async-start(), calls=%async_computation.3 | async-start | bytes 8388608 | tf_op jit(solution)/shard_map/psum | solution.py:12
  8.2 3.4 copy-start.7
  8.2 8.9 %copy-start.6 = (s32[1,1,4]{2,1,0:T(1,128)S(1)}, s32[1,1,4]{2,1,0:T(1,128)}, u32[]{:S(2)}) copy-start(s32[1,1,4]{2,1,0:T(1,128)} %param.9) | copy-start | bytes 52
  8.2 98.0 %copy-start.8 = (s32[1,1,4]{2,1,0:T(1,128)S(1)}, s32[1,1,4]{2,1,0:T(1,128)}, u32[]{:S(2)}) copy-start(s32[1,1,4]{2,1,0:T(1,128)} %param.10) | copy-start | bytes 52
  12.5 342.0 %all-to-all-start.1 = ((s32[4,2,1]{1,2,0:T(1,128)}), s32[4,2,1]{1,2,0:T(1,128)S(1)}, u32[]{:S(2)}, u32[]{:S(2)}) async-start(s32[4,2,1]{1,2,0:T(1,128)} %bitcast.71), calls=%async_computation.1 | async-start | bytes 4096 | tf_op jit(solution)/shard_map/all_to_all | solution.py:66
  312.7 5.7 %copy-start.2 = (f32[4,4,256,256]{3,2,1,0:T(8,128)S(1)}, f32[4,4,256,256]{3,2,1,0:T(8,128)}, u32[]{:S(2)}) copy-start(f32[4,4,256,256]{3,2,1,0:T(8,128)} %gather_fusion.5) | copy-start | bytes 12582916
  312.7 5.7 %copy-start.5 = (f32[4,256,256]{2,1,0:T(8,128)S(1)}, f32[4,256,256]{2,1,0:T(8,128)}, u32[]{:S(2)}) copy-start(f32[4,256,256]{2,1,0:T(8,128)} %get-tuple-element.14) | copy-start | bytes 3145732
  322.3 5.9 %copy-start.1 = (f32[4,4,256,256]{3,2,1,0:T(8,128)S(1)}, f32[4,4,256,256]{3,2,1,0:T(8,128)}, u32[]{:S(2)}) copy-start(f32[4,4,256,256]{3,2,1,0:T(8,128)} %gather_fusion.1) | copy-start | bytes 12582916
  322.3 5.9 %copy-start.4 = (f32[4,256,256]{2,1,0:T(8,128)S(1)}, f32[4,256,256]{2,1,0:T(8,128)}, u32[]{:S(2)}) copy-start(f32[4,256,256]{2,1,0:T(8,128)} %get-tuple-element.16) | copy-start | bytes 3145732
  328.2 4.4 %copy-start = (f32[4,4,256,256]{3,2,1,0:T(8,128)S(1)}, f32[4,4,256,256]{3,2,1,0:T(8,128)}, u32[]{:S(2)}) copy-start(f32[4,4,256,256]{3,2,1,0:T(8,128)} %gather_fusion.7) | copy-start | bytes 12582916
  328.2 4.4 %copy-start.3 = (f32[4,256,256]{2,1,0:T(8,128)S(1)}, f32[4,256,256]{2,1,0:T(8,128)}, u32[]{:S(2)}) copy-start(f32[4,256,256]{2,1,0:T(8,128)} %get-tuple-element.13) | copy-start | bytes 3145732
  354.6 29.6 %all-to-all-start = ((f32[8,256,256]{2,1,0:T(8,128)}), f32[8,256,256]{2,1,0:T(8,128)S(1)}, u32[]{:S(2)}, u32[]{:S(2)}) async-start(f32[8,256,256]{2,1,0:T(8,128)} %copy.82), calls=%async_computation | async-start | bytes 4194304 | tf_op jit(solution)/shard_map/all_to_all | solution.py:65
Sparse Core Ops, SparseCore 0:
  11.2 275.1 all-gather.1
Sparse Core Ops, SparseCore 1:
  11.6 120.2 all-reduce.4
where the time goes:
time: 404 us; the launch traced here: 400 us
  waiting for transfers between devices  205 us (51%)
  blocking collectives  91.8 us (23%)
  matrix products  44.9 us (11%)
  local copies, waits for them, and re-layouts  26.8 us (7%)
  between operations  15.3 us (4%)
  starting transfers between devices  9.35 us (2%)
  other arithmetic  5.93 us (1%)
    all_gather x1, waiting for transfers between devices, on_device(): lax.all_gather(matrix_tiles, 'col', axis=1, tiled=True)  180 us
    all_gather x1, blocking collectives, on_device(): lax.all_gather(tile_rows, 'col', axis=1, tiled=True)  81.7 us
    all_to_all x1, waiting for transfers between devices, on_device(): lax.all_to_all(outgoing, 'row', split_axis=0, concat_axis=0, tiled=True)  24.5 us
    dot_general x4, matrix products, section_product(): jnp.einsum('jzyl,jzyac->ljac', selector, products, precision=lax.Precisio...  23.9 us
    gather x4, local copies, waits for them, and re-layouts, section_product(): chosen = jnp.take(a_panel, columns, axis=0)  19.8 us
    dot_general x4, matrix products, section_product(): jnp.einsum('jzyab,jzbc->jzyac', chosen, b_panel, precision=lax.Precision....  19 us
  transfers between devices with their start and end apart: 4, of which 2 were waited for; matrix products, arithmetic and copies ran while one was open for 19% of the time, Pallas kernels for 0%

commit v1 on v0

v1 whole, which is shorter than its diff:
```python
import functools

import jax
import jax.numpy as jnp
from jax import lax
from jax.experimental import pallas as pl
from jax.experimental.pallas import tpu as pltpu
from jax.sharding import PartitionSpec as P

MESH = pl.DeviceIdType.MESH
TILE = 256
TR = 8
CHUNKS = 4
ROWS = TILE // CHUNKS
PIECES = 2
DONE = 32


class Copies:
    def __init__(self, send_sems, recv_sems):
        self.send_sems, self.recv_sems, self.made = send_sems, recv_sems, []

    def start(self, src, dst, device):
        number = len(self.made)
        copy = pltpu.make_async_remote_copy(
            src_ref=src,
            dst_ref=dst,
            send_sem=self.send_sems.at[number],
            recv_sem=self.recv_sems.at[number],
            device_id=device,
            device_id_type=MESH,
        )
        copy.start()
        self.made.append(copy)
        return copy

    def finish(self):
        for copy in self.made:
            copy.wait_send()


REMOTE = 3 + 7 + 3 + PIECES * (3 + 3 + 4) + CHUNKS * (9 + 4 + 3) + 3
LOCAL = 1 + CHUNKS + PIECES * 2 + 2


def kernel(
    tiles, meta, owners, out, totals,
    plane_meta, column_meta, plane_scalars, column_scalars, places,
    a_land, a_hi, a_lo, b_own, b_land, b_hi, b_lo,
    partial, far, near, inflated, outgoing, sums,
    send_sems, recv_sems, local_sems,
):
    row, col = lax.axis_index("row"), lax.axis_index("col")
    yl, core = row // 2, row % 2
    z, yh, x = col // 8, (col // 4) % 2, col % 4
    mine = yh * 4 + x

    def in_plane(dy, dx):
        return (row, z * 8 + ((yh + dy) % 2) * 4 + (x + dx) % 4)

    def in_row(dyl, dc):
        return (((yl + dyl) % 2) * 2 + (core + dc) % 2, col)

    def in_z(d):
        return (row, ((z + d) % 4) * 8 + mine)

    plane = [(dy, dx) for dy in range(2) for dx in range(4) if (dy, dx) != (0, 0)]
    rows = [(0, 1), (1, 0), (1, 1)]
    partners = [in_plane(*p) for p in plane] + [in_row(*p) for p in rows] + [in_z(d) for d in (1, 2, 3)]
    barrier = pltpu.get_barrier_semaphore()
    for device in partners:
        pl.semaphore_signal(barrier, inc=1, device_id=device, device_id_type=MESH)
    pl.semaphore_wait(barrier, len(partners))

    copies = Copies(send_sems, recv_sems)
    local_count = [0]

    def local(src, dst):
        copy = pltpu.make_async_copy(src, dst, local_sems.at[local_count[0]])
        local_count[0] += 1
        copy.start()
        return copy

    right, left, across = in_plane(0, 1), in_plane(0, 3), in_plane(1, 0)
    b_right, b_left = yh * 4 + (x + 1) % 4, yh * 4 + (x + 3) % 4
    b_across = (1 - yh) * 4 + x
    b_across_right, b_across_left = (1 - yh) * 4 + (x + 1) % 4, (1 - yh) * 4 + (x + 3) % 4

    def chunk(h):
        return pl.ds(h * ROWS, ROWS)

    a = [dict() for _ in range(CHUNKS)]

    def a_own(h):
        src = tiles.at[:, chunk(h)]
        a[h]["right"] = copies.start(src, a_land.at[h, mine], right)
        a[h]["left"] = copies.start(src, a_land.at[h, mine], left)
        a[h]["across"] = copies.start(src, a_land.at[h, mine], across)
        a[h]["self"] = local(src, a_land.at[h, mine])

    def a_pass_own(h):
        a[h]["right"].wait_recv()
        block = a_land.at[h, b_left, pl.ds(0, 2)]
        a[h]["right2"] = copies.start(block, block, right)
        a[h]["left"].wait_recv()
        block = a_land.at[h, b_right, pl.ds(2, 2)]
        a[h]["left2"] = copies.start(block, block, left)

    def a_across(h):
        a[h]["across"].wait_recv()
        block = a_land.at[h, b_across]
        a[h]["aright"] = copies.start(block, block, right)
        a[h]["aleft"] = copies.start(block, block, left)

    def a_pass_across(h):
        a[h]["aright"].wait_recv()
        block = a_land.at[h, b_across_left, pl.ds(0, 2)]
        a[h]["aright2"] = copies.start(block, block, right)
        a[h]["aleft"].wait_recv()
        block = a_land.at[h, b_across_right, pl.ds(2, 2)]
        a[h]["aleft2"] = copies.start(block, block, left)

    def a_ready(h):
        a[h]["self"].wait()
        for name in ("right2", "left2", "aright2", "aleft2"):
            a[h][name].wait_recv()

    own_meta = local(meta, column_meta.at[z, row])
    meta_row = [copies.start(meta, column_meta.at[z, row], in_row(*p)) for p in rows]
    meta_plane = [copies.start(meta, plane_meta.at[mine], in_plane(*p)) for p in plane]
    plane_meta[mine] = meta[...]
    a_own(0)

    b_row, b_self = [], []
    for p in range(PIECES):
        step = 2 // PIECES
        piece = pl.ds(p * step, step)
        b_row.append([
            copies.start(
                tiles.at[pl.ds(2 * ((core + dc) % 2) + p * step, step)],
                b_own.at[row, piece],
                in_row(dyl, dc),
            )
            for dyl, dc in rows
        ])
        b_self.append(local(tiles.at[pl.ds(2 * core + p * step, step)], b_own.at[row, piece]))
    if CHUNKS > 1:
        a_own(1)

    own_meta.wait()
    for copy in meta_row:
        copy.wait_recv()
    meta_z = [copies.start(column_meta.at[z], column_meta.at[z], in_z(d)) for d in (1, 2, 3)]

    a_pass_own(0)
    a_across(0)
    b_z, b_here = [], []
    for p in range(PIECES):
        step = 2 // PIECES
        piece = pl.ds(p * step, step)
        place = pl.ds(2 * core + p * step, step)
        for copy in b_row[p]:
            copy.wait_recv()
        b_self[p].wait()
        b_z.append([
            copies.start(b_own.at[(z + d) % 4, piece], b_land.at[z, place], in_z(d)) for d in (1, 3, 2)
        ])
        b_here.append(local(b_own.at[z, piece], b_land.at[z, place]))
        if p == 0:
            a_pass_across(0)

    for copy in meta_plane + meta_z:
        copy.wait_recv()
    to_scalars = [local(plane_meta, plane_scalars), local(column_meta, column_scalars)]
    for copy in to_scalars:
        copy.wait()
    for d in range(4):
        zc = (z + d) % 4
        for slot in range(4):
            level = column_scalars[zc, z, 0, slot]
            for m in range(4):
                keep = column_scalars[zc, row, 0, 4 + m]
                place = jnp.int32(DONE)
                for t in range(4):
                    found = plane_scalars[level, 0, t] == keep
                    place = jnp.where(found, level * 4 + t, place)
                places[(d * 4 + slot) * 4 + m] = place

    if CHUNKS > 1:
        a_pass_own(1)
        a_across(1)

    b_share = []
    for p in range(PIECES):
        step = 2 // PIECES
        place = pl.ds(2 * core + p * step, step)
        b_here[p].wait()
        block = b_land.at[z, place]
        b_share.append(copies.start(block, block, in_row(0, 1)))
        for copy, d in zip(b_z[p], (1, 3, 2)):
            copy.wait_recv()
            block = b_land.at[(z + 4 - d) % 4, place]
            b_share.append(copies.start(block, block, in_row(0, 1)))
    for copy in b_share:
        copy.wait_recv()
    for d in range(4):
        for slot in range(4):
            value = b_land[(z + d) % 4, slot]
            high = value.astype(jnp.bfloat16)
            b_hi[d * 4 + slot] = high
            b_lo[d * 4 + slot] = (value - high.astype(jnp.float32)).astype(jnp.bfloat16)
    a_hi[DONE] = jnp.zeros((ROWS, TILE), jnp.bfloat16)
    a_lo[DONE] = jnp.zeros((ROWS, TILE), jnp.bfloat16)
    inflated[4] = jnp.zeros((ROWS, TILE), jnp.float32)

    def products(h, d):
        total = jnp.zeros((4 * ROWS, TILE), jnp.float32)
        for slot in range(4):
            where = [places[(d * 4 + slot) * 4 + m] for m in range(4)]
            high = jnp.concatenate([a_hi[w] for w in where], axis=0)
            low = jnp.concatenate([a_lo[w] for w in where], axis=0)
            right_high, right_low = b_hi[d * 4 + slot], b_lo[d * 4 + slot]
            total += jnp.dot(high, right_high, preferred_element_type=jnp.float32)
            total += jnp.dot(low, right_high, preferred_element_type=jnp.float32)
            total += jnp.dot(high, right_low, preferred_element_type=jnp.float32)
        partial[h, d] = total.reshape(4, ROWS, TILE)

    column_sum = jnp.zeros((8, TILE), jnp.float32)
    slots = []
    for owner in range(4):
        first, second = jnp.int32(4), jnp.int32(4)
        for m in (3, 2, 1, 0):
            hit = owners[m] == owner
            second = jnp.where(hit, first, second)
            first = jnp.where(hit, m, first)
        slots += [first, second]

    sent_out = []
    for h in range(CHUNKS):
        a_ready(h)
        for b in range(TR):
            for t in range(4):
                value = a_land[h, b, t]
                high = value.astype(jnp.bfloat16)
                a_hi[b * 4 + t] = high
                a_lo[b * 4 + t] = (value - high.astype(jnp.float32)).astype(jnp.bfloat16)
        products(h, 2)
        far_up = copies.start(partial.at[h, 2, pl.ds(0, 2)], far.at[h, 0], in_z(1))
        far_down = copies.start(partial.at[h, 2, pl.ds(2, 2)], far.at[h, 1], in_z(3))
        if h + 1 < CHUNKS:
            a_pass_across(h + 1)
        products(h, 1)
        products(h, 3)
        if h + 2 < CHUNKS:
            a_own(h + 2)
        far_up.wait_recv()
        partial[h, 1, 0:2] = partial[h, 1, 0:2] + far[h, 0]
        near_up = copies.start(partial.at[h, 1], near.at[h, 0], in_z(1))
        far_down.wait_recv()
        partial[h, 3, 2:4] = partial[h, 3, 2:4] + far[h, 1]
        near_down = copies.start(partial.at[h, 3], near.at[h, 1], in_z(3))
        products(h, 0)
        if h + 2 < CHUNKS:
            a_pass_own(h + 2)
            a_across(h + 2)
        near_up.wait_recv()
        near_down.wait_recv()
        for m in range(4):
            value = partial[h, 0, m] + near[h, 0, m] + near[h, 1, m]
            value = value * value
            inflated[m] = value
            column_sum = column_sum + jnp.sum(value.reshape(ROWS // 8, 8, TILE), axis=0)
        for owner in range(4):
            for n in range(2):
                outgoing[h, owner, n] = inflated[slots[owner * 2 + n]]
        for dyl, dc in rows:
            device = in_row(dyl, dc)
            sent_out.append(copies.start(
                outgoing.at[h, device[0]], out.at[pl.ds(2 * row, 2), chunk(h)], device
            ))
        out[pl.ds(2 * row, 2), chunk(h)] = outgoing[h, row]

    sums[row] = column_sum
    sums_out = [copies.start(sums.at[row], sums.at[row], in_row(*p)) for p in rows]
    for copy in sums_out:
        copy.wait_recv()
    total = sums[0] + sums[1] + sums[2] + sums[3]
    totals[...] = jnp.broadcast_to(jnp.sum(total, axis=0, keepdims=True), (8, TILE))
    for copy in sent_out:
        copy.wait_recv()
    copies.finish()


def on_device(matrix_tiles, tile_rows, keep_rows, owners):
    meta = jnp.concatenate([tile_rows[0, 0], keep_rows[0, 0]])
    meta = jnp.broadcast_to(jnp.pad(meta, (0, 120))[None], (8, 128))
    f32, bf16 = jnp.float32, jnp.bfloat16
    arrived, totals = pl.pallas_call(
        kernel,
        out_shape=(
            jax.ShapeDtypeStruct((8, TILE, TILE), f32),
            jax.ShapeDtypeStruct((8, TILE), f32),
        ),
        in_specs=[
            pl.BlockSpec(memory_space=pl.ANY),
            pl.BlockSpec(memory_space=pltpu.VMEM),
            pl.BlockSpec(memory_space=pltpu.SMEM),
        ],
        out_specs=[pl.BlockSpec(memory_space=pltpu.VMEM)] * 2,
        scratch_shapes=[
            pltpu.VMEM((8, 8, 128), jnp.int32),
            pltpu.VMEM((4, 4, 8, 128), jnp.int32),
            pltpu.SMEM((8, 8, 128), jnp.int32),
            pltpu.SMEM((4, 4, 8, 128), jnp.int32),
            pltpu.SMEM((64,), jnp.int32),
            pltpu.VMEM((CHUNKS, 8, 4, ROWS, TILE), f32),
            pltpu.VMEM((33, ROWS, TILE), bf16),
            pltpu.VMEM((33, ROWS, TILE), bf16),
            pltpu.VMEM((4, 2, TILE, TILE), f32),
            pltpu.VMEM((4, 4, TILE, TILE), f32),
            pltpu.VMEM((16, TILE, TILE), bf16),
            pltpu.VMEM((16, TILE, TILE), bf16),
            pltpu.VMEM((CHUNKS, 4, 4, ROWS, TILE), f32),
            pltpu.VMEM((CHUNKS, 2, 2, ROWS, TILE), f32),
            pltpu.VMEM((CHUNKS, 2, 4, ROWS, TILE), f32),
            pltpu.VMEM((5, ROWS, TILE), f32),
            pltpu.VMEM((CHUNKS, 4, 2, ROWS, TILE), f32),
            pltpu.VMEM((4, 8, TILE), f32),
            pltpu.SemaphoreType.DMA((REMOTE,)),
            pltpu.SemaphoreType.DMA((REMOTE,)),
            pltpu.SemaphoreType.DMA((LOCAL,)),
        ],
        compiler_params=pltpu.CompilerParams(
            collective_id=0, has_side_effects=True, vmem_limit_bytes=56 << 20
        ),
        name="expand",
    )(matrix_tiles[0, 0], meta, owners[0, :, 0])
    order = float(matrix_tiles.shape[3] * 32)
    owned = order * arrived / totals[0][None, None, :]
    return owned[None, None]


def solution(mesh):
    placed = (
        P("row", "col", None, None, None),
        P("row", "col", None),
        P("row", "col", None),
        P("row", "col", None),
    )
    return jax.shard_map(
        on_device,
        mesh=mesh,
        in_specs=placed,
        out_specs=P("row", "col", None, None, None),
        check_vma=False,
    )
```

time: 404 us -> 129 us (0.32)
  waiting for transfers between devices: 205 us -> 0 us
  Pallas kernels: 0 us -> 123 us
  blocking collectives: 91.8 us -> 0 us
  matrix products: 44.9 us -> 0 us
  local copies, waits for them, and re-layouts: 26.8 us -> 1.3 us
  between operations: 15.3 us -> 0.01 us
  starting transfers between devices: 9.35 us -> 0 us
    all_gather x1 -> x0, waiting for transfers between devices: 180 us -> none  [on_device(): lax.all_gather(matrix_tiles, 'col', axis=1, tiled=True)]
    pallas_call x0 -> x1, Pallas kernels: none -> 123 us  [on_device(): pl.pallas_call(kernel, out_shape=(jax.ShapeDtypeStruct((8, TILE, TILE), f...]
    all_gather x1 -> x0, blocking collectives: 81.7 us -> none  [on_device(): lax.all_gather(tile_rows, 'col', axis=1, tiled=True)]
    dot_general x10 -> x0, matrix products: 44.9 us -> none  [the longest x4 23.9 us: section_product(): jnp.einsum('jzyl,jzyac->ljac', selector, products, precision=lax.Precisio...]
    all_to_all x2 -> x0, waiting for transfers between devices: 24.5 us -> none  [the longest x1 24.5 us: on_device(): lax.all_to_all(outgoing, 'row', split_axis=0, concat_axis=0, tiled=True)]
    gather x9 -> x0, local copies, waits for them, and re-layouts: 22.6 us -> none  [the longest x4 19.8 us: section_product(): chosen = jnp.take(a_panel, columns, axis=0)]
    psum x2 -> x0, blocking collectives: 10.1 us -> none  [the longest x1 5.87 us: on_device(): totals = lax.psum(partial_sums, 'row')]
    all_to_all x2 -> x0, starting transfers between devices: 9.31 us -> none  [the longest x1 4.78 us: on_device(): lax.all_to_all(outgoing, 'row', split_axis=0, concat_axis=0, tiled=True)]
  transfers between devices with their start and end apart: 4 -> 0, of which waited for: 2 -> 0; matrix products, arithmetic and copies ran while one was open for 19% -> 0% of each run, Pallas kernels for 0% -> 0%
where the time goes in v1:
time: 129 us
  Pallas kernels  123 us (95%)
  other arithmetic  3.89 us (3%)
  local copies, waits for them, and re-layouts  1.3 us (1%)
    pallas_call x1, Pallas kernels, on_device(): pl.pallas_call(kernel, out_shape=(jax.ShapeDtypeStruct((8, TILE, TILE), f...  123 us
    broadcast_in_dim x1, other arithmetic, on_device(): return owned[None, None]  3.14 us

profile of v1, /device:TPU:1, one launch (start us, length us, event | category | flops | bytes accessed | tf_op | source)
XLA Modules:
  0.0 128.6 jit_solution(8085090414447923999)
XLA Ops:
  0.0 0.7 pad_add_fusion
  0.8 0.6 broadcast_in_dim.4.meta
  1.3 123.4 %expand.1 = (f32[8,256,256]{2,1,0:T(8,128)}, f32[8,256]{1,0:T(8,128)}) custom-call(f32[4,256,256]{2,1,0:T(8,128)} %bitcast.7, s32[8,128]{1,0:T(8,128)} %broadcast_in_dim.4.meta, s32[4]{0:T(128)} %bitcast.9), custom_call_target="tpu_custom_call" | custom-call | tf_op jit(solution)/shard_map/expand/pallas_call | solution.py:298
  124.7 0.7 slice.3
  125.4 3.1 %divide_bitcast_fusion = f32[1,1,8,256,256]{4,3,2,1,0:T(8,128)} fusion(f32[8,256,256]{2,1,0:T(8,128)} %get-tuple-element.7, f32[256]{0:T(256)S(1)} %bitcast.8), kind=kLoop, calls=%fused_computation | loop fusion | flops 1048576 | bytes 4195328 | tf_op jit(solution)/shard_map/broadcast_in_dim | solution.py:340
  (1 shorter events, 0.0 us)

commit v2 on v1

v2 whole, which is shorter than its diff:
```python
import functools

import jax
import jax.numpy as jnp
from jax import lax
from jax.experimental import pallas as pl
from jax.experimental.pallas import tpu as pltpu
from jax.sharding import PartitionSpec as P

MESH = pl.DeviceIdType.MESH
TILE = 256
TR = 8
SIZES = (64, 64, 64, 64)
CHUNKS = len(SIZES)
STARTS = tuple(sum(SIZES[:h]) for h in range(CHUNKS))
MOST = max(SIZES)
PIECES = 4
DONE = 32
ORDER = (
    "own 0",
    "own_across 0",
    "b_column 0",
    "own 1",
    "b_column 1",
    "b_column 2",
    "b_column 3",
    "own_across 1",
    "own_across 2",
    "own_across 3",
    "meta",
    "clear",
    "slots",
    "pass_own 0",
    "across 0",
    "own 2",
    "pass_own 1",
    "b_to_planes 0",
    "own 3",
    "b_to_planes 1",
    "pass_across 0",
    "b_to_planes 2",
    "pass_own 2",
    "places",
    "b_to_planes 3",
    "b_to_core 0",
    "b_to_core 1",
    "b_to_core 2",
    "pass_own 3",
    "across 1",
    "b_to_core 3",
    "across 2",
    "b_split",
    "pass_across 1",
    "split 0",
    "far 0",
    "next 0",
    "last 0",
    "across 3",
    "near 0",
    "pass_across 2",
    "split 1",
    "far 1",
    "next 1",
    "last 1",
    "finish 0",
    "near 1",
    "pass_across 3",
    "split 2",
    "far 2",
    "next 2",
    "last 2",
    "finish 1",
    "near 2",
    "split 3",
    "far 3",
    "next 3",
    "last 3",
    "finish 2",
    "near 3",
    "finish 3",
)


class Copies:
    def __init__(self, send_sems, recv_sems):
        self.send_sems, self.recv_sems, self.made = send_sems, recv_sems, []

    def start(self, src, dst, device):
        number = len(self.made)
        copy = pltpu.make_async_remote_copy(
            src_ref=src,
            dst_ref=dst,
            send_sem=self.send_sems.at[number],
            recv_sem=self.recv_sems.at[number],
            device_id=device,
            device_id_type=MESH,
        )
        copy.start()
        self.made.append(copy)
        return copy

    def finish(self):
        for copy in self.made:
            copy.wait_send()


REMOTE = 3 + 7 + 3 + PIECES * (3 + 3 + 4) + CHUNKS * (9 + 4 + 3) + 3
LOCAL = 1 + CHUNKS + PIECES * 2 + 2


def kernel(
    tiles, tile_rows, keep_rows, owners, out, totals,
    meta, plane_meta, column_meta, plane_scalars, column_scalars, places,
    a_land, a_hi, a_lo, b_own, b_land, b_hi, b_lo,
    partial, near, inflated, outgoing, sums,
    send_sems, recv_sems, local_sems,
):
    row, col = lax.axis_index("row"), lax.axis_index("col")
    yl, core = row // 2, row % 2
    z, yh, x = col // 8, (col // 4) % 2, col % 4
    mine = yh * 4 + x

    def in_plane(dy, dx):
        return (row, z * 8 + ((yh + dy) % 2) * 4 + (x + dx) % 4)

    def in_row(dyl, dc):
        return (((yl + dyl) % 2) * 2 + (core + dc) % 2, col)

    def in_z(d):
        return (row, ((z + d) % 4) * 8 + mine)

    plane = [(dy, dx) for dy in range(2) for dx in range(4) if (dy, dx) != (0, 0)]
    rows = [(0, 1), (1, 0), (1, 1)]
    partners = [in_plane(*p) for p in plane] + [in_row(*p) for p in rows] + [in_z(d) for d in (1, 2, 3)]
    barrier = pltpu.get_barrier_semaphore()
    for device in partners:
        pl.semaphore_signal(barrier, inc=1, device_id=device, device_id_type=MESH)
    pl.semaphore_wait(barrier, len(partners))

    copies = Copies(send_sems, recv_sems)
    local_count = [0]

    def local(src, dst):
        copy = pltpu.make_async_copy(src, dst, local_sems.at[local_count[0]])
        local_count[0] += 1
        copy.start()
        return copy

    right, left, across = in_plane(0, 1), in_plane(0, 3), in_plane(1, 0)
    b_right, b_left = yh * 4 + (x + 1) % 4, yh * 4 + (x + 3) % 4
    b_across = (1 - yh) * 4 + x
    b_across_right, b_across_left = (1 - yh) * 4 + (x + 1) % 4, (1 - yh) * 4 + (x + 3) % 4

    def chunk(h):
        return pl.ds(STARTS[h], SIZES[h])

    a = [dict() for _ in range(CHUNKS)]

    def land(h, block, tiles_of=slice(None)):
        return a_land.at[block, tiles_of, chunk(h)]

    def a_own(h):
        src = tiles.at[:, chunk(h)]
        a[h]["right"] = copies.start(src, land(h, mine), right)
        a[h]["left"] = copies.start(src, land(h, mine), left)
        a[h]["self"] = local(src, land(h, mine))

    def a_own_across(h):
        a[h]["across"] = copies.start(tiles.at[:, chunk(h)], land(h, mine), across)

    def a_pass_own(h):
        a[h]["right"].wait_recv()
        block = land(h, b_left, pl.ds(0, 2))
        a[h]["right2"] = copies.start(block, block, right)
        a[h]["left"].wait_recv()
        block = land(h, b_right, pl.ds(2, 2))
        a[h]["left2"] = copies.start(block, block, left)

    def a_across(h):
        a[h]["across"].wait_recv()
        block = land(h, b_across)
        a[h]["aright"] = copies.start(block, block, right)
        a[h]["aleft"] = copies.start(block, block, left)

    def a_pass_across(h):
        a[h]["aright"].wait_recv()
        block = land(h, b_across_left, pl.ds(0, 2))
        a[h]["aright2"] = copies.start(block, block, right)
        a[h]["aleft"].wait_recv()
        block = land(h, b_across_right, pl.ds(2, 2))
        a[h]["aleft2"] = copies.start(block, block, left)

    def a_ready(h):
        a[h]["self"].wait()
        for name in ("right2", "left2", "aright2", "aleft2"):
            a[h][name].wait_recv()

    meta[0:1, 0:4] = tile_rows[...]
    meta[1:2, 0:4] = keep_rows[...]
    own_meta = local(meta, column_meta.at[z, row])
    meta_row = [copies.start(meta, column_meta.at[z, row], in_row(*p)) for p in rows]
    meta_plane = [copies.start(meta, plane_meta.at[mine], in_plane(*p)) for p in plane]
    plane_meta[mine] = meta[...]

    depth = TILE // PIECES
    b_row, b_self, b_z, b_here, b_share, meta_z = [], [], [], [], [], []

    def b_column(p):
        piece = pl.ds(p * depth, depth)
        b_row.append([
            copies.start(
                tiles.at[pl.ds(2 * ((core + dc) % 2), 2), piece], b_own.at[row, :, piece], in_row(dyl, dc)
            )
            for dyl, dc in rows
        ])
        b_self.append(local(tiles.at[pl.ds(2 * core, 2), piece], b_own.at[row, :, piece]))

    def b_place(plane_of, p):
        return b_land.at[plane_of, pl.ds(2 * core, 2), pl.ds(p * depth, depth)]

    def b_to_planes(p):
        piece = pl.ds(p * depth, depth)
        for copy in b_row[p]:
            copy.wait_recv()
        b_self[p].wait()
        b_z.append([
            copies.start(b_own.at[(z + d) % 4, :, piece], b_place(z, p), in_z(d)) for d in (2, 1, 3)
        ])
        b_here.append(local(b_own.at[z, :, piece], b_place(z, p)))

    def b_to_core(p):
        b_here[p].wait()
        b_share.append(copies.start(b_place(z, p), b_place(z, p), in_row(0, 1)))
        for copy, d in zip(b_z[p], (2, 1, 3)):
            copy.wait_recv()
            block = b_place((z + 4 - d) % 4, p)
            b_share.append(copies.start(block, block, in_row(0, 1)))

    def b_split():
        for copy in b_share:
            copy.wait_recv()
        for d in range(4):
            for slot in range(4):
                value = b_land[(z + d) % 4, slot]
                high = value.astype(jnp.bfloat16)
                b_hi[d * 4 + slot] = high
                b_lo[d * 4 + slot] = (value - high.astype(jnp.float32)).astype(jnp.bfloat16)

    def find_places():
        for copy in meta_plane + meta_z:
            copy.wait_recv()
        to_scalars = [local(plane_meta, plane_scalars), local(column_meta, column_scalars)]
        for copy in to_scalars:
            copy.wait()
        for d in range(4):
            zc = (z + d) % 4
            for slot in range(4):
                level = column_scalars[zc, z, 0, slot]
                for m in range(4):
                    keep = column_scalars[zc, row, 1, m]
                    place = jnp.int32(DONE)
                    for t in range(4):
                        found = plane_scalars[level, 0, t] == keep
                        place = jnp.where(found, level * 4 + t, place)
                    places[(d * 4 + slot) * 4 + m] = place

    def meta_to_planes():
        own_meta.wait()
        for copy in meta_row:
            copy.wait_recv()
        for d in (1, 2, 3):
            meta_z.append(copies.start(column_meta.at[z], column_meta.at[z], in_z(d)))

    def products(h, d):
        size = SIZES[h]
        total = jnp.zeros((4 * size, TILE), jnp.float32)
        for slot in range(4):
            where = [places[(d * 4 + slot) * 4 + m] for m in range(4)]
            high = jnp.concatenate([a_hi[w, 0:size] for w in where], axis=0)
            low = jnp.concatenate([a_lo[w, 0:size] for w in where], axis=0)
            right_high, right_low = b_hi[d * 4 + slot], b_lo[d * 4 + slot]
            total += jnp.dot(high, right_high, preferred_element_type=jnp.float32)
            total += jnp.dot(low, right_high, preferred_element_type=jnp.float32)
            total += jnp.dot(high, right_low, preferred_element_type=jnp.float32)
        partial[d, :, chunk(h)] = total.reshape(4, size, TILE)

    slots, sent_out, column_sums = [], [], []
    c = [dict() for _ in range(CHUNKS)]

    def find_slots():
        for owner in range(4):
            first, second = jnp.int32(4), jnp.int32(4)
            for m in (3, 2, 1, 0):
                hit = owners[m] == owner
                second = jnp.where(hit, first, second)
                first = jnp.where(hit, m, first)
            slots.extend([first, second])

    def clear():
        a_hi[DONE] = jnp.zeros((MOST, TILE), jnp.bfloat16)
        a_lo[DONE] = jnp.zeros((MOST, TILE), jnp.bfloat16)
        inflated[4] = jnp.zeros((MOST, TILE), jnp.float32)

    def a_split(h):
        a_ready(h)
        for b in range(TR):
            for t in range(4):
                value = a_land[b, t, chunk(h)]
                high = value.astype(jnp.bfloat16)
                a_hi[b * 4 + t, 0:SIZES[h]] = high
                a_lo[b * 4 + t, 0:SIZES[h]] = (value - high.astype(jnp.float32)).astype(jnp.bfloat16)

    def c_send(h, d):
        products(h, d)
        c[h][d] = copies.start(partial.at[d, :, chunk(h)], near.at[{1: 0, 3: 1, 2: 2}[d], :, chunk(h)], in_z(d))

    def c_far(h):
        products(h, 2)
        here = chunk(h)
        c[h]["up"] = copies.start(partial.at[2, pl.ds(0, 2), here], near.at[2, pl.ds(0, 2), here], in_z(1))
        c[h]["down"] = copies.start(partial.at[2, pl.ds(2, 2), here], near.at[2, pl.ds(2, 2), here], in_z(3))

    def c_next(h):
        products(h, 1)
        products(h, 3)

    def c_near(h):
        here = chunk(h)
        c[h]["up"].wait_recv()
        partial[1, 0:2, here] = partial[1, 0:2, here] + near[2, 0:2, here]
        c[h][1] = copies.start(partial.at[1, :, here], near.at[0, :, here], in_z(1))
        c[h]["down"].wait_recv()
        partial[3, 2:4, here] = partial[3, 2:4, here] + near[2, 2:4, here]
        c[h][3] = copies.start(partial.at[3, :, here], near.at[1, :, here], in_z(3))

    def c_own(h):
        products(h, 0)

    def c_finish(h):
        size, here = SIZES[h], chunk(h)
        for d in (1, 3, 2):
            if d in c[h]:
                c[h][d].wait_recv()
        column_sum = jnp.zeros((8, TILE), jnp.float32)
        for m in range(4):
            value = partial[0, m, here] + near[0, m, here] + near[1, m, here]
            if 2 in c[h]:
                value = value + near[2, m, here]
            value = value * value
            inflated[m, 0:size] = value
            column_sum = column_sum + jnp.sum(value.reshape(size // 8, 8, TILE), axis=0)
        column_sums.append(column_sum)
        for owner in range(4):
            for n in range(2):
                outgoing[owner, n, here] = inflated[slots[owner * 2 + n], 0:size]
        for dyl, dc in rows:
            device = in_row(dyl, dc)
            sent_out.append(copies.start(
                outgoing.at[device[0], :, here], out.at[pl.ds(2 * row, 2), here], device
            ))
        out[pl.ds(2 * row, 2), here] = outgoing[row, :, here]

    steps = dict(
        own=a_own, own_across=a_own_across, pass_own=a_pass_own, across=a_across, pass_across=a_pass_across,
        b_column=b_column, b_to_planes=b_to_planes, b_to_core=b_to_core, b_split=b_split, meta=meta_to_planes,
        places=find_places, slots=find_slots, clear=clear,
        split=a_split, send=c_send, far=c_far, next=c_next, near=c_near, last=c_own, finish=c_finish,
    )
    for step_of in ORDER:
        name, *numbers = step_of.split()
        steps[name](*[int(n) for n in numbers])

    sums[row] = functools.reduce(jnp.add, column_sums)
    sums_out = [copies.start(sums.at[row], sums.at[row], in_row(*p)) for p in rows]
    for copy in sums_out:
        copy.wait_recv()
    total = sums[0] + sums[1] + sums[2] + sums[3]
    totals[...] = jnp.sum(total, axis=0, keepdims=True)
    for copy in sent_out:
        copy.wait_recv()
    copies.finish()


def on_device(matrix_tiles, tile_rows, keep_rows, owners):
    f32, bf16 = jnp.float32, jnp.bfloat16
    arrived, totals = pl.pallas_call(
        kernel,
        out_shape=(
            jax.ShapeDtypeStruct((8, TILE, TILE), f32),
            jax.ShapeDtypeStruct((1, TILE), f32),
        ),
        in_specs=[
            pl.BlockSpec(memory_space=pl.ANY),
            pl.BlockSpec(memory_space=pltpu.VMEM),
            pl.BlockSpec(memory_space=pltpu.VMEM),
            pl.BlockSpec(memory_space=pltpu.SMEM),
        ],
        out_specs=[pl.BlockSpec(memory_space=pltpu.VMEM)] * 2,
        scratch_shapes=[
            pltpu.VMEM((8, 128), jnp.int32),
            pltpu.VMEM((8, 8, 128), jnp.int32),
            pltpu.VMEM((4, 4, 8, 128), jnp.int32),
            pltpu.SMEM((8, 8, 128), jnp.int32),
            pltpu.SMEM((4, 4, 8, 128), jnp.int32),
            pltpu.SMEM((64,), jnp.int32),
            pltpu.VMEM((8, 4, TILE, TILE), f32),
            pltpu.VMEM((33, MOST, TILE), bf16),
            pltpu.VMEM((33, MOST, TILE), bf16),
            pltpu.VMEM((4, 2, TILE, TILE), f32),
            pltpu.VMEM((4, 4, TILE, TILE), f32),
            pltpu.VMEM((16, TILE, TILE), bf16),
            pltpu.VMEM((16, TILE, TILE), bf16),
            pltpu.VMEM((4, 4, TILE, TILE), f32),
            pltpu.VMEM((3, 4, TILE, TILE), f32),
            pltpu.VMEM((5, MOST, TILE), f32),
            pltpu.VMEM((4, 2, TILE, TILE), f32),
            pltpu.VMEM((4, 8, TILE), f32),
            pltpu.SemaphoreType.DMA((REMOTE,)),
            pltpu.SemaphoreType.DMA((REMOTE,)),
            pltpu.SemaphoreType.DMA((LOCAL,)),
        ],
        compiler_params=pltpu.CompilerParams(
            collective_id=0, has_side_effects=True, vmem_limit_bytes=56 << 20
        ),
        name="expand",
    )(matrix_tiles[0, 0], tile_rows[0], keep_rows[0], owners[0, :, 0])
    order = float(matrix_tiles.shape[3] * 32)
    owned = order * arrived / totals[0][None, None, :]
    return owned[None, None]


def solution(mesh):
    placed = (
        P("row", "col", None, None, None),
        P("row", "col", None),
        P("row", "col", None),
        P("row", "col", None),
    )
    return jax.shard_map(
        on_device,
        mesh=mesh,
        in_specs=placed,
        out_specs=P("row", "col", None, None, None),
        check_vma=False,
    )
```

time: 129 us -> 111 us (0.86)
  Pallas kernels: 123 us -> 108 us
  local copies, waits for them, and re-layouts: 1.3 us -> 0 us
    pallas_call x1, Pallas kernels: 123 us -> 108 us  [on_device(): pl.pallas_call(kernel, out_shape=(jax.ShapeDtypeStruct((8, TILE, TILE), f...]
where the time goes in v2:
time: 111 us
  Pallas kernels  108 us (97%)
  other arithmetic  3.15 us (3%)
    pallas_call x1, Pallas kernels, on_device(): pl.pallas_call(kernel, out_shape=(jax.ShapeDtypeStruct((8, TILE, TILE), f...  108 us
    broadcast_in_dim x1, other arithmetic, on_device(): return owned[None, None]  3.15 us

profile of v2, /device:TPU:1, one launch (start us, length us, event | category | flops | bytes accessed | tf_op | source)
XLA Modules:
  0.0 111.3 jit_solution(8541529823745208136)
XLA Ops:
  0.0 108.2 %expand.1 = (f32[8,256,256]{2,1,0:T(8,128)}, f32[1,256]{1,0:T(1,128)}) custom-call(f32[4,256,256]{2,1,0:T(8,128)} %bitcast.7, s32[1,4]{1,0:T(1,128)} %bitcast.9, s32[1,4]{1,0:T(1,128)} %bitcast.10, s32[4]{0:T(128)} %bitcast.11), custom_call_target="tpu_custom_call" | custom-call | tf_op jit(solution)/shard_map/expand/pallas_call | solution.py:386
  108.2 3.2 %divide_bitcast_fusion = f32[1,1,8,256,256]{4,3,2,1,0:T(8,128)} fusion(f32[8,256,256]{2,1,0:T(8,128)} %get-tuple-element.7, f32[256]{0:T(256)} %bitcast.8), kind=kLoop, calls=%fused_computation | loop fusion | flops 1048576 | bytes 4195328 | tf_op jit(solution)/shard_map/broadcast_in_dim | solution.py:429
